TPU v7x, 32 devices: a whole 2x2x4 slice. The times are simulated.
32 devices in a mesh: blk: 16 (over z, y, x), grp: 2 (over core).
Axes of the slice: x: 2, y: 2, z: 4, core: 2. Of those that a mesh axis runs over, the one named last changes fastest.
Arguments:
- points: bfloat16 [64, 4096], P(None, ('blk', 'grp')), may hold values from -6 to 6
- right_side: float32 [16, 4096], P(None, ('blk', 'grp')), may hold values from -18 to 18
- lengthscale: float32 [1], replicated, may hold values from 3.3110573 to 4.0550324
- outputscale: float32 [1], replicated, may hold values from 0.6 to 1.6
- noise_level: float32 [1], replicated, may hold values from 0.4 to 1
Outputs:
- solution: float32 [16, 4096], P(None, ('blk', 'grp'))
- residual: float32 [16, 4096], P(None, ('blk', 'grp'))
- gradient: float32 [3], replicated
All inputs are finite; a program needn't handle non-finite values.
Results may differ from a plain program's by a relative error of at most 0.001.
The roundings to bfloat16 on the way count: a program that leaves them out, or rounds other values in their place, can miss the bound.
Values may be sent and summed in bfloat16 or wider, within the bound.
No kernel may reach another device: no remote copies, remote signals or barrier semaphores. Data moves between devices by JAX's collectives and lax.ppermute only.
A program may use at most 64 MiB of HBM per device.

v0:
```python
import functools
import math

import jax
import jax.numpy as jnp
from jax import lax
from jax.experimental import pallas as pl
from jax.experimental.pallas import tpu as pltpu
from jax.sharding import PartitionSpec as P

F32 = jnp.float32
BF16 = jnp.bfloat16
LOG2E = math.log2(math.e)
TINY = 1e-36
NT = (((1,), (1,)), ((), ()))


def _vmem(count):
    return [pl.BlockSpec(memory_space=pltpu.VMEM) for _ in range(count)]


def _smem():
    return pl.BlockSpec(memory_space=pltpu.SMEM)


def _hbm(count):
    return [pl.BlockSpec(memory_space=pltpu.HBM) for _ in range(count)]


def lane_sum(values):
    return jnp.sum(values, axis=1, keepdims=True)


def unrolled(count, most):
    return max(divisor for divisor in range(1, most + 1) if count % divisor == 0)


def pack_kernel(points_hbm, right_hbm, out_ref, points_ref, right_ref, sems):
    feats = points_ref.shape[0]
    cols = right_ref.shape[0]
    copies = [
        pltpu.make_async_copy(right_hbm, right_ref, sems.at[0]),
        pltpu.make_async_copy(points_hbm, points_ref, sems.at[1]),
    ]
    for copy in copies:
        copy.start()
    copies[0].wait()
    right = right_ref[...]
    high = right.astype(BF16)
    out_ref[feats : feats + cols, :] = high
    out_ref[feats + cols : feats + 2 * cols, :] = (right - high.astype(F32)).astype(BF16)
    copies[1].wait()
    out_ref[0:feats, :] = points_ref[...]


def fan_kernel(length_ref, amplitude_ref, jitter_ref, *refs):
    *shards, out_ref, scalars_ref = refs
    for slot, scalar in enumerate((length_ref, amplitude_ref, jitter_ref)):
        scalars_ref[slot : slot + 1, :] = jnp.full((1, 128), scalar[0], F32)
    shards = [shard[...] for shard in shards]
    for peer in range(out_ref.shape[0]):
        for side, shard in enumerate(shards):
            out_ref[peer, side] = shard


def own_place():
    return lax.axis_index("blk"), lax.axis_index("grp")


def source_of(place, paired, steps, part, step, side):
    if not paired:
        return step * 2 + side
    block, own_core = place
    core = own_core if part == 0 else 1 - own_core
    first = jnp.where((block < steps) == (side == 0), 0, steps)
    return (first + (step ^ (step >> 1))) * 2 + core


def joined(sums):
    return functools.reduce(jnp.add, [functools.reduce(jnp.add, sides) for sides in sums])


def own_operand(points_ref, scale):
    own = points_ref.shape[1]
    points = points_ref[...].astype(F32).T
    squares = jnp.sum(points * points, axis=1, keepdims=True) * ((5.0 * LOG2E * LOG2E) / (scale * scale))
    return (-2.0 * points).astype(BF16), jnp.broadcast_to(squares, (own, own))


class Distances:
    def __init__(self, scale, points, squares):
        self.scale = scale
        self.factor = (5.0 * LOG2E * LOG2E) / (scale * scale)
        self.points = points
        self.squares = squares

    def __call__(self, points):
        wide = points.astype(F32)
        squares = jnp.sum(wide * wide, axis=0, keepdims=True) * self.factor
        inner = jnp.dot(self.points, points, preferred_element_type=F32)
        reduced = jnp.maximum((self.squares + squares) + inner * self.factor, TINY)
        return reduced, reduced * lax.rsqrt(reduced)


def kern_tile(reduced, root):
    shifted = root + 1.5 * LOG2E
    return (shifted * shifted + 0.75 * LOG2E * LOG2E) * jnp.exp2(-math.log2(3.0 * LOG2E * LOG2E) - root)


def kern_kernel(has_before, with_message, scalars_ref, points_ref, *refs):
    scale = scalars_ref[0:1, :]
    refs = list(refs)
    squares_ref = refs.pop(0) if has_before else None
    part_ref = refs.pop(0)
    before = refs.pop(0)[...] if has_before else None
    right_ref = refs.pop(0) if with_message else None
    if has_before:
        distances = Distances(scale, points_ref[...], squares_ref[...])
    else:
        operand_ref, squares_ref = refs.pop(0), refs.pop(0)
        operand, squares = own_operand(points_ref, scale)
        operand_ref[...] = operand
        squares_ref[...] = squares
        distances = Distances(scale, operand, squares)
    tiles_ref, *outs = refs
    total_ref = outs[0]
    cols, own = total_ref.shape
    feats = part_ref.shape[2] - 2 * cols
    steps, sides = part_ref.shape[:2]
    total = before if has_before else jnp.zeros((cols, own), F32)

    def one_pair(step, total):
        vectors = []
        for side in range(sides):
            tile = kern_tile(*distances(part_ref[step, side, 0:feats, :]))
            tiles_ref[step, :, pl.ds(side * own, own)] = tile.astype(BF16)
            vectors.append(part_ref[step, side, feats : feats + cols, :])
        vectors = jnp.concatenate(vectors, axis=1)
        return total + lax.dot_general(vectors, tiles_ref[step], NT, preferred_element_type=F32)

    total = lax.fori_loop(0, steps, one_pair, total, unroll=unrolled(steps, 8))
    total_ref[...] = total
    if with_message:
        right = right_ref[...]
        high = right.astype(BF16).astype(F32)
        low = (right - high).astype(BF16).astype(F32)
        lost = ((right - high) - low) / jnp.where(right == 0.0, 1.0, right)
        product = total - total * lost
        message_ref = outs[1]
        rows = message_ref.shape[1]
        for peer in range(message_ref.shape[0]):
            first = (peer * rows) % cols
            message_ref[peer] = product[first : first + rows]


def dkern_kernel(has_before, scalars_ref, operand_ref, squares_ref, part_ref, *refs):
    before = refs[0][...] if has_before else None
    tiles_ref, wide_ref, total_ref, norm_ref = refs[1 if has_before else 0 :]
    cols, own = total_ref.shape
    feats = part_ref.shape[2] - 2 * cols
    distances = Distances(scalars_ref[0:1, :], operand_ref[...], squares_ref[...])
    slope = 1.0 / (3.0 * LOG2E * LOG2E * LOG2E * distances.scale)
    steps, sides = part_ref.shape[:2]
    zero = jnp.zeros((cols, own), F32)

    def one_pair(step, carried):
        total, norm = carried
        norm = list(norm)
        vectors = []
        for side in range(sides):
            reduced, root = distances(part_ref[step, side, 0:feats, :])
            tile = (reduced * slope) * ((root + LOG2E) * jnp.exp2(-root))
            tiles_ref[step, :, pl.ds(side * own, own)] = tile.astype(BF16)
            high = part_ref[step, side, feats : feats + cols, :]
            low = part_ref[step, side, feats + cols : feats + 2 * cols, :]
            right = high.astype(F32) + low.astype(F32)
            wide_ref[step, side] = right
            norm[side] = norm[side] + right * right
            vectors.append(high)
        vectors = jnp.concatenate(vectors, axis=1)
        total = total + lax.dot_general(vectors, tiles_ref[step], NT, preferred_element_type=F32)
        return total, tuple(norm)

    start = (before if has_before else zero, (zero,) * sides)
    total, norm = lax.fori_loop(0, steps, one_pair, start, unroll=unrolled(steps, 8))
    total_ref[...] = total
    norm_ref[...] = jnp.broadcast_to(lane_sum(functools.reduce(jnp.add, norm)), norm_ref.shape)


def from_lanes(row, first, cols):
    lanes = lax.broadcasted_iota(jnp.int32, (cols, 128), 1)
    rows = lax.broadcasted_iota(jnp.int32, (cols, 128), 0)
    picked = jnp.where(lanes == rows + first, jnp.broadcast_to(row, (cols, 128)), 0.0)
    return lane_sum(picked)


def into_columns(columns, cols):
    lanes = lax.broadcasted_iota(jnp.int32, (cols, 128), 1)
    kept = jnp.zeros((cols, 128), F32)
    for slot, column in enumerate(columns):
        kept = jnp.where(lanes == slot, jnp.broadcast_to(column, (cols, 128)), kept)
    return kept


def second_kernel(
    part_count, paired, scalars_ref, right_ref, kernel_ref, slope_ref,
    *refs
):
    kerns, dkerns, wides, norms, received, outs = [
        refs[group * part_count : (group + 1) * part_count] for group in range(5)
    ] + [refs[5 * part_count :]]
    (
        message_ref, direction_ref, residual_ref, applied_ref, columns_ref, products_ref, turned_ref,
    ) = outs
    cols, own = right_ref.shape
    sides = wides[0].shape[1]
    amplitude = scalars_ref[1:2, :]
    jitter = scalars_ref[2:3, :]
    place = own_place()
    low_core = place[1] == 0
    zero = jnp.zeros((cols, own), F32)
    norm = functools.reduce(jnp.add, [norm_ref[:, 0:1] for norm_ref in norms])
    steps = kerns[0].shape[0]

    sums = []
    for part in range(part_count):
        def first_pass(index, carried, part=part):
            carried = [list(sums) for sums in carried]
            for side in range(sides):
                source = source_of(place, paired, steps, part, index, side)
                product = received[0][source]
                if paired:
                    other = received[1][source]
                    product = jnp.concatenate(
                        [jnp.where(low_core, product, other), jnp.where(low_core, other, product)],
                        axis=0,
                    )
                products_ref[part * steps + index, side] = product
                right = wides[part][index, side]
                applied = amplitude * product + jitter * right
                carried[0][side] = carried[0][side] + right * applied
                carried[1][side] = carried[1][side] + applied * applied
            return tuple(tuple(sums) for sums in carried)

        sums.append(
            lax.fori_loop(0, steps, first_pass, ((zero,) * sides,) * 2, unroll=unrolled(steps, 8))
        )
    curvature, length = [lane_sum(joined(parts)) for parts in zip(*sums)]
    step = norm / curvature
    turn = (step * step * length - norm) / norm
    right_factor = jnp.broadcast_to(1.0 - step * jitter, (cols, own))
    product_factor = jnp.broadcast_to(step * amplitude, (cols, own))

    sums = []
    total = zero
    slopes = zero
    for part in range(part_count):
        def second_pass(index, carried, part=part):
            total, slopes, lengths = carried
            lengths = list(lengths)
            rounded = []
            for side in range(sides):
                right = wides[part][index, side]
                product = products_ref[part * steps + index, side]
                residual = right * right_factor - product * product_factor
                direction = residual + turn * right
                turned_ref[part * steps + index, side] = direction
                lengths[side] = lengths[side] + residual * residual
                rounded.append(direction)
            rounded = jnp.concatenate(rounded, axis=1).astype(BF16)
            tiles = jnp.concatenate([kerns[part][index], dkerns[part][index]], axis=0)
            both = lax.dot_general(rounded, tiles, NT, preferred_element_type=F32)
            total = total + both[:, 0:own]
            slopes = slopes + both[:, own : 2 * own]
            return total, slopes, tuple(lengths)

        total, slopes, lengths = lax.fori_loop(
            0, steps, second_pass, (total, slopes, (zero,) * sides), unroll=unrolled(steps, 8)
        )
        sums.append(lengths)
    norm_next = lane_sum(joined(sums))

    right = right_ref[...]
    residual = right * right_factor - kernel_ref[...] * product_factor
    direction = residual + turn * right
    applied = amplitude * total + jitter * direction
    direction_ref[...] = direction
    residual_ref[...] = residual
    applied_ref[...] = applied
    columns_ref[...] = into_columns([step, norm_next, norm, turn], cols)

    low = right - right.astype(BF16).astype(F32)
    low_direction = direction - direction.astype(BF16).astype(F32)
    slope = slope_ref[...]
    lanes = lax.broadcasted_iota(jnp.int32, (cols, 128), 1)
    rows = lax.broadcasted_iota(jnp.int32, (cols, 128), 0)
    packed = jnp.zeros((cols, 128), F32)
    for slot, values in enumerate([
        direction * applied, low * total, low * kernel_ref[...], right * slope, right * slopes,
    ]):
        packed = jnp.where(lanes == rows + slot * cols, lane_sum(values), packed)
    rows = jnp.where(rows == 0, 5 * cols, 128)
    for slot, values in enumerate([
        direction * slope, direction * slopes, low_direction * kernel_ref[...], low_direction * total,
    ]):
        packed = jnp.where(lanes == rows + slot, lane_sum(values), packed)
    packed = jnp.sum(packed, axis=0, keepdims=True)
    for peer in range(message_ref.shape[0]):
        message_ref[peer, 0:1, :] = packed
        message_ref[peer, 1:2, :] = total[0:1, :]


def last_kernel(
    part_count, paired, points_total, scalars_ref, right_ref, direction_ref,
    residual_ref, applied_ref, columns_ref, products_ref, turned_ref, received_ref, *refs
):
    wides = refs[:part_count]
    solution_hbm, final_hbm, gradient_hbm, solution_ref, final_ref, gradient_ref, sems = refs[part_count:]
    cols, own = right_ref.shape
    amplitude = scalars_ref[1:2, 0:1]
    place = own_place()
    devices = received_ref.shape[0]

    def gather_sums(device, carried):
        return carried + received_ref[device, 0:1, :]

    sums = lax.fori_loop(
        0, devices, gather_sums, jnp.zeros((1, 128), F32), unroll=unrolled(devices, 32)
    )
    step, norm_next, norm = [columns_ref[:, slot : slot + 1] for slot in range(3)]
    step_next = norm_next / from_lanes(sums, 0, cols)

    solution_ref[...] = step * right_ref[...] + step_next * direction_ref[...]
    final_ref[...] = residual_ref[...] - step_next * applied_ref[...]
    copies = [
        pltpu.make_async_copy(solution_ref, solution_hbm, sems.at[0]),
        pltpu.make_async_copy(final_ref, final_hbm, sems.at[1]),
    ]
    for copy in copies:
        copy.start()

    low_next, low_first, right_slope, right_slope_next = [
        from_lanes(sums, slot * cols, cols) for slot in range(1, 5)
    ]
    slope_cross, slope_square, low_second, low_square = [
        sums[:, 5 * cols + slot : 5 * cols + slot + 1] for slot in range(4)
    ]
    turn = columns_ref[:, 3:4]
    dots = turn * norm
    squares = norm_next + turn * dots
    steps, sides = wides[0].shape[:2]
    zero = jnp.zeros((cols, own), F32)
    row_zero = jnp.zeros((1, own), F32)
    sums = []
    for part in range(part_count):
        def one_pair(index, carried, part=part):
            carried = [list(sums) for sums in carried]
            block = part * steps + index
            for side in range(sides):
                vector = step * wides[part][index, side] + step_next * turned_ref[block, side]
                rounded = vector.astype(BF16).astype(F32)
                source = source_of(place, paired, steps, part, index, side)
                carried[0][side] = carried[0][side] + products_ref[block, side] * rounded
                carried[1][side] = carried[1][side] + received_ref[source, 1:2, :] * rounded[0:1, :]
            return tuple(tuple(sums) for sums in carried)

        start = ((zero,) * sides, (row_zero,) * sides)
        sums.append(lax.fori_loop(0, steps, one_pair, start, unroll=unrolled(steps, 4)))
    whole, first_row = [joined(parts) for parts in zip(*sums)]
    right_kernel = lane_sum(whole) + step * low_first + step_next * low_next
    first_step, second_step = step[0:1], step_next[0:1]
    direction_kernel = lane_sum(first_row) + first_step * low_second + second_step * low_square
    direction_slope = first_step * slope_cross + second_step * slope_square
    is_first = lax.broadcasted_iota(jnp.int32, (cols, 1), 0) == 0
    weight = jnp.where(is_first, 1.0, -1.0 / (cols - 1))
    for slot, (right_form, direction_form) in enumerate((
        (
            amplitude * (step * right_slope + step_next * right_slope_next),
            amplitude * direction_slope,
        ),
        (right_kernel, direction_kernel),
        (step * norm + step_next * dots, (step * dots + step_next * squares)[0:1]),
    )):
        form = jnp.where(is_first, step * right_form + step_next * direction_form, right_form)
        gradient_ref[slot] = jnp.sum(weight * form) * (0.5 / points_total)
    copies.append(pltpu.make_async_copy(gradient_ref, gradient_hbm, sems.at[2]))
    copies[2].start()
    for copy in copies:
        copy.wait()


SWAP = [(0, 1), (1, 0)]


def local(mesh_shape, points, right_side, lengthscale, outputscale, noise_level):
    axes = ("blk", "grp")
    feats, own = points.shape
    cols = right_side.shape[0]
    rows = feats + 2 * cols
    blocks = mesh_shape["blk"]
    devices = blocks * mesh_shape["grp"]
    paired = mesh_shape["grp"] == 2 and blocks >= 2 and blocks & (blocks - 1) == 0
    part_count = 2 if paired else 1
    steps = devices // (2 * part_count)
    params = pltpu.CompilerParams(vmem_limit_bytes=(4 << 20) + devices * (40 << 10))
    shape = pltpu.VMEM
    result = jax.ShapeDtypeStruct

    def near(*arrays):
        return [pltpu.with_memory_space_constraint(array, pltpu.VMEM) for array in arrays]

    call = functools.partial(pl.pallas_call, compiler_params=params)

    row_shape = shape((cols, own), F32)
    shard, own_points, own_right = call(
        pack_kernel,
        out_shape=(shape((rows, own), BF16), shape((feats, own), BF16), row_shape),
        in_specs=_hbm(2),
        out_specs=tuple(_vmem(3)),
        scratch_shapes=[pltpu.SemaphoreType.DMA((2,))],
        name="pack",
    )(*[pltpu.with_memory_space_constraint(array, pltpu.HBM) for array in (points, right_side)])
    shards = [shard]
    if paired:
        half = blocks // 2
        shards.append(lax.ppermute(shard, "blk", [(at, (at + half) % blocks) for at in range(blocks)]))
    peers = blocks // 2 if paired else devices
    message, scalars = call(
        fan_kernel,
        out_shape=(shape((peers, len(shards), rows, own), BF16), shape((8, 128), F32)),
        in_specs=[_smem()] * 3 + _vmem(len(shards)),
        out_specs=tuple(_vmem(2)),
        name="fan",
    )(lengthscale, outputscale, noise_level, *near(*shards))
    if paired:
        groups = [
            [2 * (side * half + (at ^ (at >> 1))) + core for at in range(half)]
            for side in range(2)
            for core in range(2)
        ]
        vectors = [lax.all_to_all(message, axes, 0, 0, tiled=True, axis_index_groups=groups)]
        vectors.append(lax.ppermute(vectors[0], "grp", SWAP))
    else:
        vectors = [lax.all_to_all(message, axes, 0, 0, tiled=True).reshape(steps, 2, rows, own)]

    tile_shape = shape((steps, own, 2 * own), BF16)
    wide_shape = shape((steps, 2, cols, own), F32)

    operands = []

    def kern_call(part, vector, *before):
        outs = [tile_shape, row_shape]
        if part == 0:
            outs = [shape((own, feats), BF16), shape((own, own), F32)] + outs
        with_message = part + 1 == part_count
        if with_message:
            outs.append(shape((devices, cols // part_count, own), F32))
            before = (*before, own_right)
        results = call(
            functools.partial(kern_kernel, part > 0, with_message),
            out_shape=tuple(outs),
            in_specs=_vmem(2 + len(operands or [vector]) + len(before)),
            out_specs=tuple(_vmem(len(outs))),
            name="kern",
        )(*near(scalars, *(operands or [own_points]), vector, *before))
        if part == 0:
            operands.extend(results[:2])
            results = results[2:]
        return results

    def dkern_call(vector, *before):
        return call(
            functools.partial(dkern_kernel, len(before) > 0),
            out_shape=(tile_shape, wide_shape, row_shape, row_shape),
            in_specs=_vmem(4 + len(before)),
            out_specs=tuple(_vmem(4)),
            name="dkern",
        )(*near(scalars, *operands, vector, *before))

    kerns = [kern_call(0, vectors[0])]
    dkerns = []
    if paired:
        dkerns.append(dkern_call(vectors[0]))
        vectors[1], *dkerns[0] = lax.optimization_barrier((vectors[1], *dkerns[0]))
        kerns.append(kern_call(1, vectors[1], kerns[0][1]))
    kernel_first, message = kerns[-1][1:]
    received = [lax.all_to_all(message, axes, 0, 0, tiled=True)]
    if paired:
        received[0], vectors[1] = lax.optimization_barrier((received[0], vectors[1]))
        received.append(lax.ppermute(received[0], "grp", SWAP))
        dkerns.append(dkern_call(vectors[1], dkerns[0][2]))
    else:
        dkerns.append(dkern_call(vectors[0]))
    kerns = [tiles for tiles, *rest in kerns]
    slope_first = dkerns[-1][2]
    dkerns, wides, norms = [[outs[slot] for outs in dkerns] for slot in (0, 1, 3)]

    both_shape = shape((devices // 2, 2, cols, own), F32)
    message, direction, residual, applied, columns, products, turned = call(
        functools.partial(second_kernel, part_count, paired),
        out_shape=(
            shape((devices, 2, own), F32), row_shape, row_shape, row_shape, shape((cols, 128), F32),
            both_shape, both_shape,
        ),
        in_specs=_vmem(4 + 5 * part_count),
        out_specs=tuple(_vmem(7)),
        name="second",
    )(
        *near(scalars, own_right, kernel_first, slope_first, *kerns, *dkerns, *wides, *norms, *received),
    )
    received = lax.all_to_all(message, axes, 0, 0, tiled=True)

    solution, final, gradient = call(
        functools.partial(last_kernel, part_count, paired, float(own * devices)),
        out_shape=(result((cols, own), F32), result((cols, own), F32), result((3,), F32)),
        in_specs=_vmem(9 + part_count),
        out_specs=tuple(_hbm(3)),
        scratch_shapes=[
            pltpu.VMEM((cols, own), F32),
            pltpu.VMEM((cols, own), F32),
            pltpu.SMEM((3,), F32),
            pltpu.SemaphoreType.DMA((3,)),
        ],
        name="last",
    )(
        *near(scalars, own_right, direction, residual, applied, columns, products, turned, received, *wides),
    )
    return solution, final, gradient


def solution(mesh):
    whole = P(None, ("blk", "grp"))
    return jax.shard_map(
        functools.partial(local, dict(mesh.shape)),
        mesh=mesh,
        in_specs=(whole, whole, P(), P(), P()),
        out_specs=(whole, whole, P()),
        check_vma=False,
    )
```

profile of v0, /device:TPU:0, one launch (start us, length us, event | category | flops | bytes accessed | tf_op | source)
XLA Modules:
  0.0 46.2 jit_solution(8514428363274180021)
XLA Ops:
  0.6 0.8 %pack.1 = (bf16[96,128]{1,0:T(8,128)(2,1)S(1)}, bf16[64,128]{1,0:T(8,128)(2,1)S(1)}, f32[16,128]{1,0:T(8,128)S(1)}) custom-call(bf16[64,128]{1,0:T(8,128)(2,1)} %points_hbm.1, f32[16,128]{1,0:T(8,128)} %right_hbm.1), custom_call_target="tpu_custom_call" | custom-call | tf_op jit(solution)/shard_map/pack/pallas_call | solution.py:415
  1.4 4.1 %collective-permute-start = (bf16[96,128]{1,0:T(8,128)(2,1)S(1)}, bf16[96,128]{1,0:T(8,128)(2,1)S(1)}, u32[]{:S(2)}, u32[]{:S(2)}) collective-permute-start(bf16[96,128]{1,0:T(8,128)(2,1)S(1)} %get-tuple-element.37.refs_0_), channel_id=1, source_target_pairs={{0,16},{2,18},{4,20},{6,22},{8,24},{10,26},{12,28},{14,30},{16,0},... | collective-permute-start | bytes 73736 | tf_op jit(solution)/shard_map/ppermute | solution.py:426
  7.5 0.0 collective-permute-done.refs_1_
  7.5 0.1 fan.1
  7.5 12.1 %all_to_all.15.refs_0_.part_ref = bf16[8,2,96,128]{3,2,1,0:T(8,128)(2,1)S(1)} all-to-all(bf16[8,2,96,128]{3,2,1,0:T(8,128)(2,1)S(1)} %get-tuple-element.41), channel_id=1, replica_groups={{0,2,6,4,12,14,10,8},{1,3,7,5,13,15,11,9},{16,18,22,20,28,30,26,24},{17..., dimensions={0} | all-to-all | bytes 786432 | tf_op jit(solution)/shard_map/all_to_all | solution.py:441
  19.6 0.0 collective-permute-start.1
  19.6 0.8 %kern.2 = (bf16[128,64]{1,0:T(8,128)(2,1)S(1)}, f32[128,128]{1,0:T(8,128)S(1)}, bf16[8,128,256]{2,1,0:T(8,128)(2,1)S(1)}, f32[16,128]{1,0:T(8,128)S(1)}) custom-call(f32[8,128]{1,0:T(8,128)S(1)} %get-tuple-element.38.scalars_ref, bf16[64,128]{1,0:T(8,128)(2,1)S(1)} %get-tuple-element.40.points_ref, bf16[8,2,96,128]{3,2,1,0:T(8,128)(2,1)S(1)} %all_to_all.15.refs_0_.part_ref), custom_call_target="tpu_custom_call" | custom-call | tf_op jit(solution)/shard_map/kern/pallas_call | solution.py:459
  20.4 0.8 %dkern.2 = (bf16[8,128,256]{2,1,0:T(8,128)(2,1)S(1)}, f32[8,2,16,128]{3,2,1,0:T(8,128)S(1)}, f32[16,128]{1,0:T(8,128)S(1)}, f32[16,128]{1,0:T(8,128)S(1)}) custom-call(f32[8,128]{1,0:T(8,128)S(1)} %get-tuple-element.38.scalars_ref, bf16[128,64]{1,0:T(8,128)(2,1)S(1)} %get-tuple-element.42.operand_ref.points_ref, ...), custom_call_target="tpu_custom_call" | custom-call | tf_op jit(solution)/shard_map/dkern/pallas_call | solution.py:472
  21.3 0.1 collective-permute-done.1.refs_1_.part_ref
  21.4 0.8 %kern.3 = (bf16[8,128,256]{2,1,0:T(8,128)(2,1)S(1)}, f32[16,128]{1,0:T(8,128)S(1)}, f32[32,8,128]{2,1,0:T(8,128)S(1)}) custom-call(f32[8,128]{1,0:T(8,128)S(1)} %get-tuple-element.38.scalars_ref, bf16[128,64]{1,0:T(8,128)(2,1)S(1)} %get-tuple-element.42.operand_ref.points_ref, f32[128,128]{1,0:T(8,128)S(1)} %get-tuple-element.43.squares_ref.refs_0_, ...), custom_call_target="tpu_custom_call" | custom-call | tf_op jit(solution)/shard_map/kern/pallas_call | solution.py:459
  22.2 11.4 %all_to_all.16.refs_8_ = f32[32,8,128]{2,1,0:T(8,128)S(1)} all-to-all(f32[32,8,128]{2,1,0:T(8,128)S(1)} %get-tuple-element.51), channel_id=1, replica_groups=mesh['blk'=16,'grp'=2] {'blk','grp'}, dimensions={0} | all-to-all | bytes 262144 | tf_op jit(solution)/shard_map/all_to_all | solution.py:487
  33.6 0.2 collective-permute-start.2
  33.8 0.8 %dkern.3 = (bf16[8,128,256]{2,1,0:T(8,128)(2,1)S(1)}, f32[8,2,16,128]{3,2,1,0:T(8,128)S(1)}, f32[16,128]{1,0:T(8,128)S(1)}, f32[16,128]{1,0:T(8,128)S(1)}) custom-call(f32[8,128]{1,0:T(8,128)S(1)} %get-tuple-element.38.scalars_ref, bf16[128,64]{1,0:T(8,128)(2,1)S(1)} %get-tuple-element.42.operand_ref.points_ref, ...), custom_call_target="tpu_custom_call" | custom-call | tf_op jit(solution)/shard_map/dkern/pallas_call | solution.py:472
  34.6 0.4 collective-permute-done.2.refs_9_
  35.0 1.0 %second.1 = (f32[32,2,128]{2,1,0:T(2,128)S(1)}, f32[16,128]{1,0:T(8,128)S(1)}, f32[16,128]{1,0:T(8,128)S(1)}, f32[16,128]{1,0:T(8,128)S(1)}, f32[16,128]{1,0:T(8...) custom-call(f32[8,128]{1,0:T(8,128)S(1)} %get-tuple-element.38.scalars_ref, ...), custom_call_target="tpu_custom_call" | custom-call | tf_op jit(solution)/shard_map/second/pallas_call | solution.py:499
  35.9 9.0 %all_to_all.17.received_ref = f32[32,2,128]{2,1,0:T(2,128)S(1)} all-to-all(f32[32,2,128]{2,1,0:T(2,128)S(1)} %get-tuple-element.70), channel_id=1, replica_groups=mesh['blk'=16,'grp'=2] {'blk','grp'}, dimensions={0} | all-to-all | bytes 65536 | tf_op jit(solution)/shard_map/all_to_all | solution.py:511
  45.0 1.2 %last.1 = (f32[16,128]{1,0:T(8,128)}, f32[16,128]{1,0:T(8,128)}, f32[3]{0:T(128)}) custom-call(f32[8,128]{1,0:T(8,128)S(1)} %get-tuple-element.38.scalars_ref, f32[16,128]{1,0:T(8,128)S(1)} %get-tuple-element.39.refs_3_.right_ref, f32[16,128]{1,0:T(8,128)S(1)} %get-tuple-element.64.direction_ref, f32[16,128]{1,0:T(8,128)S(1)} %get-tuple-element.65.residual_ref, ...), custom_call_target="tpu_custom_call" | custom-call | tf_op jit(solution)/shard_map/last/pallas_call | solution.py:513
Async XLA Ops:
  1.4 6.1 %collective-permute-start = (bf16[96,128]{1,0:T(8,128)(2,1)S(1)}, bf16[96,128]{1,0:T(8,128)(2,1)S(1)}, u32[]{:S(2)}, u32[]{:S(2)}) collective-permute-start(bf16[96,128]{1,0:T(8,128)(2,1)S(1)} %get-tuple-element.37.refs_0_), channel_id=1, source_target_pairs={{0,16},{2,18},{4,20},{6,22},{8,24},{10,26},{12,28},{14,30},{16,0},... | collective-permute-start | bytes 73736 | tf_op jit(solution)/shard_map/ppermute | solution.py:426
  19.6 1.7 %collective-permute-start.1 = (bf16[8,2,96,128]{3,2,1,0:T(8,128)(2,1)S(1)}, bf16[8,2,96,128]{3,2,1,0:T(8,128)(2,1)S(1)}, u32[]{:S(2)}, u32[]{:S(2)}) collective-permute-start(bf16[8,2,96,128]{3,2,1,0:T(8,128)(2,1)S(1)} %all_to_all.15.refs_0_.part_ref), channel_id=1, source_target_pairs={{0,1},{1,0},{2,3},{3,2},{4,5},{5,4},{6,7},{7,6},{8,9},{9,8},{10,11... | collective-permute-start | bytes 1179656 | tf_op jit(solution)/shard_map/ppermute | solution.py:442
  33.6 1.3 %collective-permute-start.2 = (f32[32,8,128]{2,1,0:T(8,128)S(1)}, f32[32,8,128]{2,1,0:T(8,128)S(1)}, u32[]{:S(2)}, u32[]{:S(2)}) collective-permute-start(f32[32,8,128]{2,1,0:T(8,128)S(1)} %all_to_all.16.refs_8_), channel_id=1, source_target_pairs={{0,1},{1,0},{2,3},{3,2},{4,5},{5,4},{6,7},{7,6},{8,9},{9,8},{10,11... | collective-permute-start | bytes 393224 | tf_op jit(solution)/shard_map/ppermute | solution.py:490
where the time goes:
time: 46.6 us; the launch traced here: 46.2 us
  blocking collectives  32.6 us (70%)
  Pallas kernels  6.23 us (13%)
  starting transfers between devices  4.35 us (9%)
  between operations  2.62 us (6%)
    all_to_all x1, blocking collectives, local(): lax.all_to_all(message, axes, 0, 0, tiled=True, axis_index_groups=groups)  12.1 us
    all_to_all x1, blocking collectives, local(): received = [lax.all_to_all(message, axes, 0, 0, tiled=True)]  11.4 us
    all_to_all x1, blocking collectives, local(): received = lax.all_to_all(message, axes, 0, 0, tiled=True)  9.02 us
    ppermute x1, starting transfers between devices, local(): lax.ppermute(shard, 'blk', [(at, (at + half) % blocks) for at in range(bl...  4.13 us
    pallas_call x2, Pallas kernels, dkern_call(): call(functools.partial(dkern_kernel, len(before) > 0), out_shape=(tile_sh...  1.62 us
    pallas_call x2, Pallas kernels, kern_call(): call(functools.partial(kern_kernel, part > 0, with_message), out_shape=tu...  1.59 us
    pallas_call x1, Pallas kernels, local(): call(functools.partial(last_kernel, part_count, paired, float(own * devic...  1.25 us
    pallas_call x1, Pallas kernels, local(): call(functools.partial(second_kernel, part_count, paired), out_shape=(sha...  0.97 us
  transfers between devices with their start and end apart: 3, of which 2 were waited for; matrix products, arithmetic and copies ran while one was open for 0% of the time, Pallas kernels for 5%

commit v1 on v0

--- a/solution.py
+++ b/solution.py
@@ -321,11 +321,19 @@
     place = own_place()
     devices = received_ref.shape[0]
 
-    def gather_sums(device, carried):
-        return carried + received_ref[device, 0:1, :]
-
-    sums = lax.fori_loop(
-        0, devices, gather_sums, jnp.zeros((1, 128), F32), unroll=unrolled(devices, 32)
+    chains = unrolled(devices, 4)
+
+    def gather_sums(group, carried):
+        return tuple(
+            sums + received_ref[group * chains + chain, 0:1, :] for chain, sums in enumerate(carried)
+        )
+
+    sums = functools.reduce(
+        jnp.add,
+        lax.fori_loop(
+            0, devices // chains, gather_sums, (jnp.zeros((1, 128), F32),) * chains,
+            unroll=unrolled(devices // chains, 8),
+        ),
     )
     step, norm_next, norm = [columns_ref[:, slot : slot + 1] for slot in range(3)]
     step_next = norm_next / from_lanes(sums, 0, cols)

time: 46.6 us -> 46.6 us (level)
  no operation moved by 1% of the time
where the time goes in v1:
time: 46.6 us; the launch traced here: 46.2 us
  blocking collectives  32.6 us (70%)
  Pallas kernels  6.22 us (13%)
  starting transfers between devices  4.35 us (9%)
  between operations  2.62 us (6%)
    all_to_all x1, blocking collectives, local(): lax.all_to_all(message, axes, 0, 0, tiled=True, axis_index_groups=groups)  12.1 us
    all_to_all x1, blocking collectives, local(): received = [lax.all_to_all(message, axes, 0, 0, tiled=True)]  11.4 us
    all_to_all x1, blocking collectives, local(): received = lax.all_to_all(message, axes, 0, 0, tiled=True)  9.02 us
    ppermute x1, starting transfers between devices, local(): lax.ppermute(shard, 'blk', [(at, (at + half) % blocks) for at in range(bl...  4.13 us
    pallas_call x2, Pallas kernels, dkern_call(): call(functools.partial(dkern_kernel, len(before) > 0), out_shape=(tile_sh...  1.62 us
    pallas_call x2, Pallas kernels, kern_call(): call(functools.partial(kern_kernel, part > 0, with_message), out_shape=tu...  1.59 us
    pallas_call x1, Pallas kernels, local(): call(functools.partial(last_kernel, part_count, paired, float(own * devic...  1.23 us
    pallas_call x1, Pallas kernels, local(): call(functools.partial(second_kernel, part_count, paired), out_shape=(sha...  0.97 us
  transfers between devices with their start and end apart: 3, of which 2 were waited for; matrix products, arithmetic and copies ran while one was open for 0% of the time, Pallas kernels for 5%

profile of v1, /device:TPU:0, one launch (start us, length us, event | category | flops | bytes accessed | tf_op | source)
XLA Modules:
  0.0 46.2 jit_solution(7746656020910095064)
XLA Ops:
  0.6 0.8 %pack.1 = (bf16[96,128]{1,0:T(8,128)(2,1)S(1)}, bf16[64,128]{1,0:T(8,128)(2,1)S(1)}, f32[16,128]{1,0:T(8,128)S(1)}) custom-call(bf16[64,128]{1,0:T(8,128)(2,1)} %points_hbm.1, f32[16,128]{1,0:T(8,128)} %right_hbm.1), custom_call_target="tpu_custom_call" | custom-call | tf_op jit(solution)/shard_map/pack/pallas_call | solution.py:423
  1.4 4.1 %collective-permute-start = (bf16[96,128]{1,0:T(8,128)(2,1)S(1)}, bf16[96,128]{1,0:T(8,128)(2,1)S(1)}, u32[]{:S(2)}, u32[]{:S(2)}) collective-permute-start(bf16[96,128]{1,0:T(8,128)(2,1)S(1)} %get-tuple-element.37.refs_0_), channel_id=1, source_target_pairs={{0,16},{2,18},{4,20},{6,22},{8,24},{10,26},{12,28},{14,30},{16,0},... | collective-permute-start | bytes 73736 | tf_op jit(solution)/shard_map/ppermute | solution.py:434
  7.5 0.0 collective-permute-done.refs_1_
  7.5 0.1 fan.1
  7.5 12.1 %all_to_all.15.refs_0_.part_ref = bf16[8,2,96,128]{3,2,1,0:T(8,128)(2,1)S(1)} all-to-all(bf16[8,2,96,128]{3,2,1,0:T(8,128)(2,1)S(1)} %get-tuple-element.41), channel_id=1, replica_groups={{0,2,6,4,12,14,10,8},{1,3,7,5,13,15,11,9},{16,18,22,20,28,30,26,24},{17..., dimensions={0} | all-to-all | bytes 786432 | tf_op jit(solution)/shard_map/all_to_all | solution.py:449
  19.6 0.0 collective-permute-start.1
  19.6 0.8 %kern.2 = (bf16[128,64]{1,0:T(8,128)(2,1)S(1)}, f32[128,128]{1,0:T(8,128)S(1)}, bf16[8,128,256]{2,1,0:T(8,128)(2,1)S(1)}, f32[16,128]{1,0:T(8,128)S(1)}) custom-call(f32[8,128]{1,0:T(8,128)S(1)} %get-tuple-element.38.scalars_ref, bf16[64,128]{1,0:T(8,128)(2,1)S(1)} %get-tuple-element.40.points_ref, bf16[8,2,96,128]{3,2,1,0:T(8,128)(2,1)S(1)} %all_to_all.15.refs_0_.part_ref), custom_call_target="tpu_custom_call" | custom-call | tf_op jit(solution)/shard_map/kern/pallas_call | solution.py:467
  20.4 0.8 %dkern.2 = (bf16[8,128,256]{2,1,0:T(8,128)(2,1)S(1)}, f32[8,2,16,128]{3,2,1,0:T(8,128)S(1)}, f32[16,128]{1,0:T(8,128)S(1)}, f32[16,128]{1,0:T(8,128)S(1)}) custom-call(f32[8,128]{1,0:T(8,128)S(1)} %get-tuple-element.38.scalars_ref, bf16[128,64]{1,0:T(8,128)(2,1)S(1)} %get-tuple-element.42.operand_ref.points_ref, ...), custom_call_target="tpu_custom_call" | custom-call | tf_op jit(solution)/shard_map/dkern/pallas_call | solution.py:480
  21.3 0.1 collective-permute-done.1.refs_1_.part_ref
  21.4 0.8 %kern.3 = (bf16[8,128,256]{2,1,0:T(8,128)(2,1)S(1)}, f32[16,128]{1,0:T(8,128)S(1)}, f32[32,8,128]{2,1,0:T(8,128)S(1)}) custom-call(f32[8,128]{1,0:T(8,128)S(1)} %get-tuple-element.38.scalars_ref, bf16[128,64]{1,0:T(8,128)(2,1)S(1)} %get-tuple-element.42.operand_ref.points_ref, f32[128,128]{1,0:T(8,128)S(1)} %get-tuple-element.43.squares_ref.refs_0_, ...), custom_call_target="tpu_custom_call" | custom-call | tf_op jit(solution)/shard_map/kern/pallas_call | solution.py:467
  22.2 11.4 %all_to_all.16.refs_8_ = f32[32,8,128]{2,1,0:T(8,128)S(1)} all-to-all(f32[32,8,128]{2,1,0:T(8,128)S(1)} %get-tuple-element.51), channel_id=1, replica_groups=mesh['blk'=16,'grp'=2] {'blk','grp'}, dimensions={0} | all-to-all | bytes 262144 | tf_op jit(solution)/shard_map/all_to_all | solution.py:495
  33.6 0.2 collective-permute-start.2
  33.8 0.8 %dkern.3 = (bf16[8,128,256]{2,1,0:T(8,128)(2,1)S(1)}, f32[8,2,16,128]{3,2,1,0:T(8,128)S(1)}, f32[16,128]{1,0:T(8,128)S(1)}, f32[16,128]{1,0:T(8,128)S(1)}) custom-call(f32[8,128]{1,0:T(8,128)S(1)} %get-tuple-element.38.scalars_ref, bf16[128,64]{1,0:T(8,128)(2,1)S(1)} %get-tuple-element.42.operand_ref.points_ref, ...), custom_call_target="tpu_custom_call" | custom-call | tf_op jit(solution)/shard_map/dkern/pallas_call | solution.py:480
  34.6 0.4 collective-permute-done.2.refs_9_
  35.0 1.0 %second.1 = (f32[32,2,128]{2,1,0:T(2,128)S(1)}, f32[16,128]{1,0:T(8,128)S(1)}, f32[16,128]{1,0:T(8,128)S(1)}, f32[16,128]{1,0:T(8,128)S(1)}, f32[16,128]{1,0:T(8...) custom-call(f32[8,128]{1,0:T(8,128)S(1)} %get-tuple-element.38.scalars_ref, ...), custom_call_target="tpu_custom_call" | custom-call | tf_op jit(solution)/shard_map/second/pallas_call | solution.py:507
  35.9 9.0 %all_to_all.17.received_ref = f32[32,2,128]{2,1,0:T(2,128)S(1)} all-to-all(f32[32,2,128]{2,1,0:T(2,128)S(1)} %get-tuple-element.70), channel_id=1, replica_groups=mesh['blk'=16,'grp'=2] {'blk','grp'}, dimensions={0} | all-to-all | bytes 65536 | tf_op jit(solution)/shard_map/all_to_all | solution.py:519
  45.0 1.2 %last.1 = (f32[16,128]{1,0:T(8,128)}, f32[16,128]{1,0:T(8,128)}, f32[3]{0:T(128)}) custom-call(f32[8,128]{1,0:T(8,128)S(1)} %get-tuple-element.38.scalars_ref, f32[16,128]{1,0:T(8,128)S(1)} %get-tuple-element.39.refs_3_.right_ref, f32[16,128]{1,0:T(8,128)S(1)} %get-tuple-element.64.direction_ref, f32[16,128]{1,0:T(8,128)S(1)} %get-tuple-element.65.residual_ref, ...), custom_call_target="tpu_custom_call" | custom-call | tf_op jit(solution)/shard_map/last/pallas_call | solution.py:521
Async XLA Ops:
  1.4 6.1 %collective-permute-start = (bf16[96,128]{1,0:T(8,128)(2,1)S(1)}, bf16[96,128]{1,0:T(8,128)(2,1)S(1)}, u32[]{:S(2)}, u32[]{:S(2)}) collective-permute-start(bf16[96,128]{1,0:T(8,128)(2,1)S(1)} %get-tuple-element.37.refs_0_), channel_id=1, source_target_pairs={{0,16},{2,18},{4,20},{6,22},{8,24},{10,26},{12,28},{14,30},{16,0},... | collective-permute-start | bytes 73736 | tf_op jit(solution)/shard_map/ppermute | solution.py:434
  19.6 1.7 %collective-permute-start.1 = (bf16[8,2,96,128]{3,2,1,0:T(8,128)(2,1)S(1)}, bf16[8,2,96,128]{3,2,1,0:T(8,128)(2,1)S(1)}, u32[]{:S(2)}, u32[]{:S(2)}) collective-permute-start(bf16[8,2,96,128]{3,2,1,0:T(8,128)(2,1)S(1)} %all_to_all.15.refs_0_.part_ref), channel_id=1, source_target_pairs={{0,1},{1,0},{2,3},{3,2},{4,5},{5,4},{6,7},{7,6},{8,9},{9,8},{10,11... | collective-permute-start | bytes 1179656 | tf_op jit(solution)/shard_map/ppermute | solution.py:450
  33.6 1.3 %collective-permute-start.2 = (f32[32,8,128]{2,1,0:T(8,128)S(1)}, f32[32,8,128]{2,1,0:T(8,128)S(1)}, u32[]{:S(2)}, u32[]{:S(2)}) collective-permute-start(f32[32,8,128]{2,1,0:T(8,128)S(1)} %all_to_all.16.refs_8_), channel_id=1, source_target_pairs={{0,1},{1,0},{2,3},{3,2},{4,5},{5,4},{6,7},{7,6},{8,9},{9,8},{10,11... | collective-permute-start | bytes 393224 | tf_op jit(solution)/shard_map/ppermute | solution.py:498

commit v2 on v1

--- a/solution.py
+++ b/solution.py
@@ -339,13 +339,13 @@
     step_next = norm_next / from_lanes(sums, 0, cols)
 
     solution_ref[...] = step * right_ref[...] + step_next * direction_ref[...]
-    final_ref[...] = residual_ref[...] - step_next * applied_ref[...]
     copies = [
         pltpu.make_async_copy(solution_ref, solution_hbm, sems.at[0]),
         pltpu.make_async_copy(final_ref, final_hbm, sems.at[1]),
     ]
-    for copy in copies:
-        copy.start()
+    copies[0].start()
+    final_ref[...] = residual_ref[...] - step_next * applied_ref[...]
+    copies[1].start()
 
     low_next, low_first, right_slope, right_slope_next = [
         from_lanes(sums, slot * cols, cols) for slot in range(1, 5)

time: 46.6 us -> 46.6 us (level)
  no operation moved by 1% of the time
where the time goes in v2:
time: 46.6 us; the launch traced here: 46.2 us
  blocking collectives  32.6 us (70%)
  Pallas kernels  6.22 us (13%)
  starting transfers between devices  4.35 us (9%)
  between operations  2.62 us (6%)
    all_to_all x1, blocking collectives, local(): lax.all_to_all(message, axes, 0, 0, tiled=True, axis_index_groups=groups)  12.1 us
    all_to_all x1, blocking collectives, local(): received = [lax.all_to_all(message, axes, 0, 0, tiled=True)]  11.4 us
    all_to_all x1, blocking collectives, local(): received = lax.all_to_all(message, axes, 0, 0, tiled=True)  9.02 us
    ppermute x1, starting transfers between devices, local(): lax.ppermute(shard, 'blk', [(at, (at + half) % blocks) for at in range(bl...  4.13 us
    pallas_call x2, Pallas kernels, dkern_call(): call(functools.partial(dkern_kernel, len(before) > 0), out_shape=(tile_sh...  1.62 us
    pallas_call x2, Pallas kernels, kern_call(): call(functools.partial(kern_kernel, part > 0, with_message), out_shape=tu...  1.59 us
    pallas_call x1, Pallas kernels, local(): call(functools.partial(last_kernel, part_count, paired, float(own * devic...  1.23 us
    pallas_call x1, Pallas kernels, local(): call(functools.partial(second_kernel, part_count, paired), out_shape=(sha...  0.97 us
  transfers between devices with their start and end apart: 3, of which 2 were waited for; matrix products, arithmetic and copies ran while one was open for 0% of the time, Pallas kernels for 5%

profile of v2, /device:TPU:0, one launch (start us, length us, event | category | flops | bytes accessed | tf_op | source)
XLA Modules:
  0.0 46.2 jit_solution(7746656020910095064)
XLA Ops:
  0.6 0.8 %pack.1 = (bf16[96,128]{1,0:T(8,128)(2,1)S(1)}, bf16[64,128]{1,0:T(8,128)(2,1)S(1)}, f32[16,128]{1,0:T(8,128)S(1)}) custom-call(bf16[64,128]{1,0:T(8,128)(2,1)} %points_hbm.1, f32[16,128]{1,0:T(8,128)} %right_hbm.1), custom_call_target="tpu_custom_call" | custom-call | tf_op jit(solution)/shard_map/pack/pallas_call | solution.py:423
  1.4 4.1 %collective-permute-start = (bf16[96,128]{1,0:T(8,128)(2,1)S(1)}, bf16[96,128]{1,0:T(8,128)(2,1)S(1)}, u32[]{:S(2)}, u32[]{:S(2)}) collective-permute-start(bf16[96,128]{1,0:T(8,128)(2,1)S(1)} %get-tuple-element.37.refs_0_), channel_id=1, source_target_pairs={{0,16},{2,18},{4,20},{6,22},{8,24},{10,26},{12,28},{14,30},{16,0},... | collective-permute-start | bytes 73736 | tf_op jit(solution)/shard_map/ppermute | solution.py:434
  7.5 0.0 collective-permute-done.refs_1_
  7.5 0.1 fan.1
  7.5 12.1 %all_to_all.15.refs_0_.part_ref = bf16[8,2,96,128]{3,2,1,0:T(8,128)(2,1)S(1)} all-to-all(bf16[8,2,96,128]{3,2,1,0:T(8,128)(2,1)S(1)} %get-tuple-element.41), channel_id=1, replica_groups={{0,2,6,4,12,14,10,8},{1,3,7,5,13,15,11,9},{16,18,22,20,28,30,26,24},{17..., dimensions={0} | all-to-all | bytes 786432 | tf_op jit(solution)/shard_map/all_to_all | solution.py:449
  19.6 0.0 collective-permute-start.1
  19.6 0.8 %kern.2 = (bf16[128,64]{1,0:T(8,128)(2,1)S(1)}, f32[128,128]{1,0:T(8,128)S(1)}, bf16[8,128,256]{2,1,0:T(8,128)(2,1)S(1)}, f32[16,128]{1,0:T(8,128)S(1)}) custom-call(f32[8,128]{1,0:T(8,128)S(1)} %get-tuple-element.38.scalars_ref, bf16[64,128]{1,0:T(8,128)(2,1)S(1)} %get-tuple-element.40.points_ref, bf16[8,2,96,128]{3,2,1,0:T(8,128)(2,1)S(1)} %all_to_all.15.refs_0_.part_ref), custom_call_target="tpu_custom_call" | custom-call | tf_op jit(solution)/shard_map/kern/pallas_call | solution.py:467
  20.4 0.8 %dkern.2 = (bf16[8,128,256]{2,1,0:T(8,128)(2,1)S(1)}, f32[8,2,16,128]{3,2,1,0:T(8,128)S(1)}, f32[16,128]{1,0:T(8,128)S(1)}, f32[16,128]{1,0:T(8,128)S(1)}) custom-call(f32[8,128]{1,0:T(8,128)S(1)} %get-tuple-element.38.scalars_ref, bf16[128,64]{1,0:T(8,128)(2,1)S(1)} %get-tuple-element.42.operand_ref.points_ref, ...), custom_call_target="tpu_custom_call" | custom-call | tf_op jit(solution)/shard_map/dkern/pallas_call | solution.py:480
  21.3 0.1 collective-permute-done.1.refs_1_.part_ref
  21.4 0.8 %kern.3 = (bf16[8,128,256]{2,1,0:T(8,128)(2,1)S(1)}, f32[16,128]{1,0:T(8,128)S(1)}, f32[32,8,128]{2,1,0:T(8,128)S(1)}) custom-call(f32[8,128]{1,0:T(8,128)S(1)} %get-tuple-element.38.scalars_ref, bf16[128,64]{1,0:T(8,128)(2,1)S(1)} %get-tuple-element.42.operand_ref.points_ref, f32[128,128]{1,0:T(8,128)S(1)} %get-tuple-element.43.squares_ref.refs_0_, ...), custom_call_target="tpu_custom_call" | custom-call | tf_op jit(solution)/shard_map/kern/pallas_call | solution.py:467
  22.2 11.4 %all_to_all.16.refs_8_ = f32[32,8,128]{2,1,0:T(8,128)S(1)} all-to-all(f32[32,8,128]{2,1,0:T(8,128)S(1)} %get-tuple-element.51), channel_id=1, replica_groups=mesh['blk'=16,'grp'=2] {'blk','grp'}, dimensions={0} | all-to-all | bytes 262144 | tf_op jit(solution)/shard_map/all_to_all | solution.py:495
  33.6 0.2 collective-permute-start.2
  33.8 0.8 %dkern.3 = (bf16[8,128,256]{2,1,0:T(8,128)(2,1)S(1)}, f32[8,2,16,128]{3,2,1,0:T(8,128)S(1)}, f32[16,128]{1,0:T(8,128)S(1)}, f32[16,128]{1,0:T(8,128)S(1)}) custom-call(f32[8,128]{1,0:T(8,128)S(1)} %get-tuple-element.38.scalars_ref, bf16[128,64]{1,0:T(8,128)(2,1)S(1)} %get-tuple-element.42.operand_ref.points_ref, ...), custom_call_target="tpu_custom_call" | custom-call | tf_op jit(solution)/shard_map/dkern/pallas_call | solution.py:480
  34.6 0.4 collective-permute-done.2.refs_9_
  35.0 1.0 %second.1 = (f32[32,2,128]{2,1,0:T(2,128)S(1)}, f32[16,128]{1,0:T(8,128)S(1)}, f32[16,128]{1,0:T(8,128)S(1)}, f32[16,128]{1,0:T(8,128)S(1)}, f32[16,128]{1,0:T(8...) custom-call(f32[8,128]{1,0:T(8,128)S(1)} %get-tuple-element.38.scalars_ref, ...), custom_call_target="tpu_custom_call" | custom-call | tf_op jit(solution)/shard_map/second/pallas_call | solution.py:507
  35.9 9.0 %all_to_all.17.received_ref = f32[32,2,128]{2,1,0:T(2,128)S(1)} all-to-all(f32[32,2,128]{2,1,0:T(2,128)S(1)} %get-tuple-element.70), channel_id=1, replica_groups=mesh['blk'=16,'grp'=2] {'blk','grp'}, dimensions={0} | all-to-all | bytes 65536 | tf_op jit(solution)/shard_map/all_to_all | solution.py:519
  45.0 1.2 %last.1 = (f32[16,128]{1,0:T(8,128)}, f32[16,128]{1,0:T(8,128)}, f32[3]{0:T(128)}) custom-call(f32[8,128]{1,0:T(8,128)S(1)} %get-tuple-element.38.scalars_ref, f32[16,128]{1,0:T(8,128)S(1)} %get-tuple-element.39.refs_3_.right_ref, f32[16,128]{1,0:T(8,128)S(1)} %get-tuple-element.64.direction_ref, f32[16,128]{1,0:T(8,128)S(1)} %get-tuple-element.65.residual_ref, ...), custom_call_target="tpu_custom_call" | custom-call | tf_op jit(solution)/shard_map/last/pallas_call | solution.py:521
Async XLA Ops:
  1.4 6.1 %collective-permute-start = (bf16[96,128]{1,0:T(8,128)(2,1)S(1)}, bf16[96,128]{1,0:T(8,128)(2,1)S(1)}, u32[]{:S(2)}, u32[]{:S(2)}) collective-permute-start(bf16[96,128]{1,0:T(8,128)(2,1)S(1)} %get-tuple-element.37.refs_0_), channel_id=1, source_target_pairs={{0,16},{2,18},{4,20},{6,22},{8,24},{10,26},{12,28},{14,30},{16,0},... | collective-permute-start | bytes 73736 | tf_op jit(solution)/shard_map/ppermute | solution.py:434
  19.6 1.7 %collective-permute-start.1 = (bf16[8,2,96,128]{3,2,1,0:T(8,128)(2,1)S(1)}, bf16[8,2,96,128]{3,2,1,0:T(8,128)(2,1)S(1)}, u32[]{:S(2)}, u32[]{:S(2)}) collective-permute-start(bf16[8,2,96,128]{3,2,1,0:T(8,128)(2,1)S(1)} %all_to_all.15.refs_0_.part_ref), channel_id=1, source_target_pairs={{0,1},{1,0},{2,3},{3,2},{4,5},{5,4},{6,7},{7,6},{8,9},{9,8},{10,11... | collective-permute-start | bytes 1179656 | tf_op jit(solution)/shard_map/ppermute | solution.py:450
  33.6 1.3 %collective-permute-start.2 = (f32[32,8,128]{2,1,0:T(8,128)S(1)}, f32[32,8,128]{2,1,0:T(8,128)S(1)}, u32[]{:S(2)}, u32[]{:S(2)}) collective-permute-start(f32[32,8,128]{2,1,0:T(8,128)S(1)} %all_to_all.16.refs_8_), channel_id=1, source_target_pairs={{0,1},{1,0},{2,3},{3,2},{4,5},{5,4},{6,7},{7,6},{8,9},{9,8},{10,11... | collective-permute-start | bytes 393224 | tf_op jit(solution)/shard_map/ppermute | solution.py:498
